TPU v7x, 128 devices: a whole 4x4x4 slice. The times are simulated.
128 devices in a mesh: pair: 2 (over core), batch: 4 (over y), vocab: 16 (over x, z).
Axes of the slice: x: 4, y: 4, z: 4, core: 2. Of those that a mesh axis runs over, the one named last changes fastest.
Arguments:
- hidden: bfloat16 [2, 512, 8192], P('pair', 'batch', 'vocab'), may hold values from -120 to 120
- norm_gain: bfloat16 [8192], P('vocab'), may hold values from 0.099609375 to 1.8984375
- head_weight: bfloat16 [8192, 65536], P(('pair', 'batch'), 'vocab'), may hold values from -1 to 1
Outputs:
- guided_logprobs: float32 [512, 65536], P(('pair', 'batch'), 'vocab')
- cond_logprobs: float32 [512, 65536], P(('pair', 'batch'), 'vocab')
All inputs are finite; a program needn't handle non-finite values.
Results may differ from a plain program's by a relative error of at most 0.007.
Values may be sent and summed in bfloat16 or wider, within the bound.
A program may use at most 128 MiB of HBM per device.

v0:
```python
import jax
import jax.numpy as jnp
from jax import lax
from jax.sharding import PartitionSpec as P

D = 8192
EPS = 1e-05
GUIDE = 1.5


def on_device(hidden, norm_gain, head_weight):
    rows = hidden[0]
    wide = rows.astype(jnp.float32)
    partial_sq = jnp.sum(wide * wide, axis=1)
    total_sq = lax.psum(partial_sq, "vocab")
    scaled = wide * lax.rsqrt(total_sq / D + EPS)[:, None] * norm_gain.astype(jnp.float32)[None, :]
    features = lax.all_gather(scaled.astype(jnp.bfloat16), "vocab", axis=1, tiled=True)
    blocks = lax.all_to_all(features, ("pair", "batch"), split_axis=1, concat_axis=0, tiled=True)
    groups = lax.axis_size("pair") * lax.axis_size("batch")
    width = blocks.shape[1]
    out_rows = blocks.shape[0] // (2 * groups)
    ordered = blocks.reshape(2, groups, out_rows, width).transpose(1, 0, 2, 3).reshape(-1, width)
    logits = lax.psum_scatter(
        jnp.dot(ordered, head_weight, preferred_element_type=jnp.float32),
        ("pair", "batch"),
        scatter_dimension=0,
        tiled=True,
    )
    cond = logits[:out_rows]
    uncond = logits[out_rows:]
    guided = GUIDE * cond + (1.0 - GUIDE) * uncond
    peak_c, peak_g = lax.pmax((jnp.max(cond, axis=1), jnp.max(guided, axis=1)), "vocab")
    local_c = jnp.sum(jnp.exp(cond - peak_c[:, None]), axis=1)
    local_g = jnp.sum(jnp.exp(guided - peak_g[:, None]), axis=1)
    total_c, total_g = lax.psum((local_c, local_g), "vocab")
    cond_out = cond - (peak_c + jnp.log(total_c))[:, None]
    guided_out = guided - (peak_g + jnp.log(total_g))[:, None]
    return (guided_out, cond_out)


def solution(mesh):
    in_specs = (P("pair", "batch", "vocab"), P("vocab"), P(("pair", "batch"), "vocab"))
    out_specs = (P(("pair", "batch"), "vocab"), P(("pair", "batch"), "vocab"))
    return jax.shard_map(
        on_device, mesh=mesh, in_specs=in_specs, out_specs=out_specs, check_vma=False
    )
```

profile of v0, /device:TPU:32, one launch (start us, length us, event | category | flops | bytes accessed | tf_op | source)
XLA Modules:
  0.0 398.5 jit_solution(13088770015210042575)
XLA Ops:
  7.2 0.0 all-gather.2.cloned.1.call-start
  7.2 0.7 convert_element_type.14
  7.9 1.0 copy.6
  8.9 0.1 fusion.1
  9.0 36.8 %psum.21 = f32[128]{0:T(128)S(1)} all-reduce(f32[128]{0:T(128)S(1)} %fusion.1), channel_id=1, replica_groups=mesh['pair'=2,'batch'=4,'vocab'=16] {'vocab'}, use_global_device_ids=true, to_apply=%region_1.0 | all-reduce | flops 128 | bytes 1024 | tf_op jit(solution)/shard_map/psum | solution.py:15
  45.9 0.8 fusion.3
  46.7 0.0 all-gather.2.cloned.1.call-update
  46.7 0.0 reduce-scatter.2.cloned.1.call-start
  46.7 45.9 %all-gather.2.cloned.1.call-done = bf16[128,8192]{0,1:T(8,128)(2,1)} async-done(((bf16[128,512]{0,1:T(8,128)(2,1)}), bf16[128,8192]{0,1:T(8,128)(2,1)}) %all-gather.2.cloned.1.call-update) | async-done | bytes 2097168 | tf_op jit(solution)/shard_map/all_gather | solution.py:17
  92.7 30.9 %all_to_all.16 = bf16[128,8,1024]{0,2,1:T(8,128)(2,1)S(1)} all-to-all(bf16[128,8,1024]{0,2,1:T(8,128)(2,1)} %bitcast.14), channel_id=1, replica_groups=mesh['pair'=2,'batch'=4,'vocab'=16] {'pair','batch'}, dimensions={1} | all-to-all | bytes 4194304 | tf_op jit(solution)/shard_map/all_to_all | solution.py:18
  123.5 2.6 copy.7
  126.1 1.8 copy.8
  127.9 14.4 %fusion.5 = f32[1024,4096]{1,0:T(8,128)} fusion(bf16[1024,1024]{1,0:T(8,128)(2,1)S(1)} %bitcast.15, bf16[1024,4096]{1,0:T(8,128)(2,1)} %param.5), kind=kOutput, calls=%fused_computation.16 | convolution fusion | flops 8589934592 | bytes 27262976 | tf_op jit(solution)/shard_map/dot_general | solution.py:24
  142.4 0.0 reduce-scatter.2.cloned.1.call-update
  142.4 168.8 %reduce-scatter.2.cloned.1.call-done = f32[128,4096]{1,0:T(8,128)} async-done(((f32[1024,4096]{1,0:T(8,128)}), f32[128,4096]{1,0:T(8,128)}) %reduce-scatter.2.cloned.1.call-update) | async-done | bytes 2097168 | tf_op jit(solution)/shard_map/reduce_scatter | solution.py:23
  311.1 0.0 copy-start
  311.1 2.0 slice_reduce_fusion
  313.1 36.4 %all-reduce.1 = (f32[64]{0:T(128)S(1)}, f32[64]{0:T(128)S(1)}) all-reduce(f32[64]{0:T(128)S(1)} %get-tuple-element.5, f32[64]{0:T(128)S(1)} %get-tuple-element.4), channel_id=1, replica_groups=mesh['pair'=2,'batch'=4,'vocab'=16] {'vocab'}, use_global_device_ids=true, to_apply=%region_4.0 | all-reduce | flops 128 | bytes 1024 | tf_op jit(solution)/shard_map/pmax | solution.py:32
  349.5 0.0 copy-done
  349.5 0.5 exponential_reduce_fusion
  350.1 40.0 %all-reduce = (f32[64]{0:T(128)S(1)}, f32[64]{0:T(128)S(1)}) all-reduce(f32[64]{0:T(128)S(1)} %get-tuple-element.3, f32[64]{0:T(128)S(1)} %get-tuple-element.2), channel_id=1, replica_groups=mesh['pair'=2,'batch'=4,'vocab'=16] {'vocab'}, use_global_device_ids=true, to_apply=%region_6.0 | all-reduce | flops 128 | bytes 1024 | tf_op jit(solution)/shard_map/psum | solution.py:35
  390.1 1.6 slice_subtract_fusion
  (2 shorter events, 0.0 us)
Async XLA Ops:
  7.2 85.5 %all-gather.2.cloned.1.call-start = ((), (), s32[]{:S(2)}) async-start(), calls=%async_computation.2 | async-start | bytes 2228224 | tf_op jit(solution)/shard_map/all_gather | solution.py:17
  46.7 264.5 %reduce-scatter.2.cloned.1.call-start = ((), (), s32[]{:S(2)}) async-start(), calls=%async_computation.3 | async-start | bytes 18874368 | tf_op jit(solution)/shard_map/reduce_scatter | solution.py:23
  311.1 38.4 %copy-start = (f32[128,4096]{1,0:T(8,128)S(1)}, f32[128,4096]{1,0:T(8,128)}, u32[]{:S(2)}) copy-start(f32[128,4096]{1,0:T(8,128)} %reduce-scatter.2.cloned.1.call-done) | copy-start | bytes 6291460
Sparse Core Ops, SparseCore 0:
  46.8 45.8 all-gather.1
  142.5 168.5 reduce-scatter.1
where the time goes:
time: 399 us
  waiting for transfers between devices  215 us (54%)
  blocking collectives  144 us (36%)
  matrix products  14.4 us (4%)
  between operations  14.1 us (4%)
  other arithmetic  5.68 us (1%)
  local copies, waits for them, and re-layouts  5.44 us (1%)
    reduce_scatter x1, waiting for transfers between devices, on_device(): lax.psum_scatter(jnp.dot(ordered, head_weight, preferred_element_type=jnp...  169 us
    all_gather x1, waiting for transfers between devices, on_device(): lax.all_gather(scaled.astype(jnp.bfloat16), 'vocab', axis=1, tiled=True)  45.9 us
    psum x1, blocking collectives, on_device(): total_c, total_g = lax.psum((local_c, local_g), 'vocab')  40 us
    psum x1, blocking collectives, on_device(): total_sq = lax.psum(partial_sq, 'vocab')  36.8 us
    pmax x1, blocking collectives, on_device(): lax.pmax((jnp.max(cond, axis=1), jnp.max(guided, axis=1)), 'vocab')  36.4 us
    all_to_all x1, blocking collectives, on_device(): lax.all_to_all(features, ('pair', 'batch'), split_axis=1, concat_axis=0,...  30.9 us
    dot_general x1, matrix products, on_device(): jnp.dot(ordered, head_weight, preferred_element_type=jnp.float32)  14.4 us
  transfers between devices with their start and end apart: 2, of which 2 were waited for; matrix products, arithmetic and copies ran while one was open for 0% of the time, Pallas kernels for 0%

commit v1 on v0

--- a/solution.py
+++ b/solution.py
@@ -12,7 +12,7 @@
     rows = hidden[0]
     wide = rows.astype(jnp.float32)
     partial_sq = jnp.sum(wide * wide, axis=1)
-    total_sq = lax.psum(partial_sq, "vocab")
+    total_sq = jnp.sum(lax.all_gather(partial_sq, "vocab"), axis=0)
     scaled = wide * lax.rsqrt(total_sq / D + EPS)[:, None] * norm_gain.astype(jnp.float32)[None, :]
     features = lax.all_gather(scaled.astype(jnp.bfloat16), "vocab", axis=1, tiled=True)
     blocks = lax.all_to_all(features, ("pair", "batch"), split_axis=1, concat_axis=0, tiled=True)

time: 399 us -> 382 us (0.957)
  blocking collectives: 144 us -> 129 us
    psum x1 -> x0, blocking collectives: 36.8 us -> none  [on_device(): total_sq = lax.psum(partial_sq, 'vocab')]
    all_gather x0 -> x1, blocking collectives: none -> 21.2 us  [on_device(): total_sq = jnp.sum(lax.all_gather(partial_sq, 'vocab'), axis=0)]
where the time goes in v1:
time: 382 us
  waiting for transfers between devices  214 us (56%)
  blocking collectives  129 us (34%)
  matrix products  14.4 us (4%)
  between operations  14.1 us (4%)
  other arithmetic  5.71 us (1%)
  local copies, waits for them, and re-layouts  5.44 us (1%)
    reduce_scatter x1, waiting for transfers between devices, on_device(): lax.psum_scatter(jnp.dot(ordered, head_weight, preferred_element_type=jnp...  169 us
    all_gather x1, waiting for transfers between devices, on_device(): lax.all_gather(scaled.astype(jnp.bfloat16), 'vocab', axis=1, tiled=True)  45.1 us
    psum x1, blocking collectives, on_device(): total_c, total_g = lax.psum((local_c, local_g), 'vocab')  40 us
    pmax x1, blocking collectives, on_device(): lax.pmax((jnp.max(cond, axis=1), jnp.max(guided, axis=1)), 'vocab')  36.4 us
    all_to_all x1, blocking collectives, on_device(): lax.all_to_all(features, ('pair', 'batch'), split_axis=1, concat_axis=0,...  30.9 us
    all_gather x1, blocking collectives, on_device(): total_sq = jnp.sum(lax.all_gather(partial_sq, 'vocab'), axis=0)  21.2 us
    dot_general x1, matrix products, on_device(): jnp.dot(ordered, head_weight, preferred_element_type=jnp.float32)  14.4 us
  transfers between devices with their start and end apart: 2, of which 2 were waited for; matrix products, arithmetic and copies ran while one was open for 0% of the time, Pallas kernels for 0%

profile of v1, /device:TPU:32, one launch (start us, length us, event | category | flops | bytes accessed | tf_op | source)
XLA Modules:
  0.0 382.1 jit_solution(992642435925621733)
XLA Ops:
  7.2 0.0 all-gather.4.cloned.1.call-start
  7.2 0.7 convert_element_type.14
  7.9 1.0 copy.9
  8.9 0.1 fusion.1
  9.0 21.2 %all-gather.1 = f32[16,1,128]{2,1,0:T(1,128)S(1)} all-gather(f32[1,1,128]{2,1,0:T(1,128)S(1)} %bitcast.17), channel_id=2, replica_groups=mesh['pair'=2,'batch'=4,'vocab'=16] {'vocab'}, dimensions={0}, use_global_device_ids=true | all-gather | bytes 8704 | tf_op jit(solution)/shard_map/all_gather | solution.py:15
  30.3 0.8 fusion.3
  31.1 0.0 all-gather.4.cloned.1.call-update
  31.1 0.0 reduce-scatter.2.cloned.1.call-start
  31.1 45.1 %all-gather.4.cloned.1.call-done = bf16[128,8192]{0,1:T(8,128)(2,1)} async-done(((bf16[128,512]{0,1:T(8,128)(2,1)}), bf16[128,8192]{0,1:T(8,128)(2,1)}) %all-gather.4.cloned.1.call-update) | async-done | bytes 2097168 | tf_op jit(solution)/shard_map/all_gather | solution.py:17
  76.2 30.9 %all_to_all.16 = bf16[128,8,1024]{0,2,1:T(8,128)(2,1)S(1)} all-to-all(bf16[128,8,1024]{0,2,1:T(8,128)(2,1)} %bitcast.15), channel_id=1, replica_groups=mesh['pair'=2,'batch'=4,'vocab'=16] {'pair','batch'}, dimensions={1} | all-to-all | bytes 4194304 | tf_op jit(solution)/shard_map/all_to_all | solution.py:18
  107.1 2.6 copy.10
  109.7 1.8 copy.11
  111.5 14.4 %fusion.5 = f32[1024,4096]{1,0:T(8,128)} fusion(bf16[1024,1024]{1,0:T(8,128)(2,1)S(1)} %bitcast.16, bf16[1024,4096]{1,0:T(8,128)(2,1)} %param.5), kind=kOutput, calls=%fused_computation.16 | convolution fusion | flops 8589934592 | bytes 27262976 | tf_op jit(solution)/shard_map/dot_general | solution.py:24
  125.9 0.0 reduce-scatter.2.cloned.1.call-update
  125.9 168.8 %reduce-scatter.2.cloned.1.call-done = f32[128,4096]{1,0:T(8,128)} async-done(((f32[1024,4096]{1,0:T(8,128)}), f32[128,4096]{1,0:T(8,128)}) %reduce-scatter.2.cloned.1.call-update) | async-done | bytes 2097168 | tf_op jit(solution)/shard_map/reduce_scatter | solution.py:23
  294.7 0.0 copy-start
  294.7 2.0 slice_reduce_fusion
  296.6 36.4 %all-reduce.1 = (f32[64]{0:T(128)S(1)}, f32[64]{0:T(128)S(1)}) all-reduce(f32[64]{0:T(128)S(1)} %get-tuple-element.5, f32[64]{0:T(128)S(1)} %get-tuple-element.4), channel_id=1, replica_groups=mesh['pair'=2,'batch'=4,'vocab'=16] {'vocab'}, use_global_device_ids=true, to_apply=%region_4.0 | all-reduce | flops 128 | bytes 1024 | tf_op jit(solution)/shard_map/pmax | solution.py:32
  333.1 0.0 copy-done
  333.1 0.5 exponential_reduce_fusion
  333.6 40.0 %all-reduce = (f32[64]{0:T(128)S(1)}, f32[64]{0:T(128)S(1)}) all-reduce(f32[64]{0:T(128)S(1)} %get-tuple-element.3, f32[64]{0:T(128)S(1)} %get-tuple-element.2), channel_id=1, replica_groups=mesh['pair'=2,'batch'=4,'vocab'=16] {'vocab'}, use_global_device_ids=true, to_apply=%region_6.0 | all-reduce | flops 128 | bytes 1024 | tf_op jit(solution)/shard_map/psum | solution.py:35
  373.6 1.6 slice_subtract_fusion
  (3 shorter events, 0.1 us)
Async XLA Ops:
  7.2 69.0 %all-gather.4.cloned.1.call-start = ((), (), s32[]{:S(2)}) async-start(), calls=%async_computation.2 | async-start | bytes 2228224 | tf_op jit(solution)/shard_map/all_gather | solution.py:17
  31.1 263.6 %reduce-scatter.2.cloned.1.call-start = ((), (), s32[]{:S(2)}) async-start(), calls=%async_computation.3 | async-start | bytes 18874368 | tf_op jit(solution)/shard_map/reduce_scatter | solution.py:23
  294.7 38.4 %copy-start = (f32[128,4096]{1,0:T(8,128)S(1)}, f32[128,4096]{1,0:T(8,128)}, u32[]{:S(2)}) copy-start(f32[128,4096]{1,0:T(8,128)} %reduce-scatter.2.cloned.1.call-done) | copy-start | bytes 6291460
Sparse Core Ops, SparseCore 0:
  31.2 44.9 all-gather.3
  126.0 168.5 reduce-scatter.1
